TPU v7x, 256 devices: a whole 4x4x8 slice. The times are simulated.
256 devices in a mesh: row: 8 (over x, core), col: 32 (over z, y).
Axes of the slice: x: 4, y: 4, z: 8, core: 2. Of those that a mesh axis runs over, the one named last changes fastest.
Arguments:
- matrix: float32 [24576, 12288], P('row', 'col'), may hold values from -6 to 6
Outputs:
- updated: float32 [24576, 12288], P('row', 'col')
All inputs are finite; a program needn't handle non-finite values.
Results may differ from a plain program's by a relative error of at most 0.0003.
Values sent between devices are 32-bit elements; how exact they have to be, the bound alone decides.
A program may use at most 64 MiB of HBM per device.

v0:
```python
import jax
import jax.numpy as jnp
from jax import lax
from jax.sharding import PartitionSpec as P

PANEL = 256
HIGHEST = lax.Precision.HIGHEST


def partner_2(block, axis, distance):
    count = lax.axis_size(axis)
    route = []
    for low in range(count):
        high = low | 1 << distance
        if high != low and high < count:
            route += [(low, high), (high, low)]
    return lax.ppermute(block, axis, route)


def broadcast(value, axis, source):
    kept = jnp.where(lax.axis_index(axis) == source, value, 0).astype(value.dtype)
    return lax.psum(kept, axis)


def upper_of(gram):
    return jnp.linalg.cholesky(gram).T


def combine_pair(upper_one, upper_two):
    gram = jnp.dot(upper_one.T, upper_one, precision=HIGHEST) + jnp.dot(
        upper_two.T, upper_two, precision=HIGHEST
    )
    return upper_of(gram)


def apply_inverse(upper, rows):
    return jax.scipy.linalg.solve_triangular(upper.T, rows.T, lower=True).T


def factor(panel):
    gram_local = lax.dot_general(panel, panel, (((0,), (0,)), ((), ())), precision=HIGHEST)
    is_first = lax.axis_index("row") == 0
    identity = jnp.eye(PANEL, dtype=jnp.float32)
    upper = upper_of(gram_local)
    for level in range(lax.axis_size("row").bit_length() - 1):
        partner = partner_2(upper, "row", level)
        upper = combine_pair(upper, partner)
    basis = apply_inverse(upper, panel)
    top_block = broadcast(basis[:PANEL], "row", 0)
    lead = identity + top_block
    vectors = basis.at[:PANEL].add(jnp.where(is_first, identity, jnp.zeros_like(identity)))
    return (vectors, lead)


def on_device(matrix):
    panel = matrix[:, :PANEL]
    vectors, lead = factor(panel)
    vectors, lead = (broadcast(vectors, "col", 0), broadcast(lead, "col", 0))
    partial_proj = lax.dot_general(vectors, matrix, (((0,), (0,)), ((), ())), precision=HIGHEST)
    projected = lax.psum(partial_proj, "row")
    lead_gram = jnp.dot(lead.T, lead, precision=HIGHEST)
    lead_factor = jnp.linalg.cholesky(lead_gram)
    coeffs = jax.scipy.linalg.cho_solve(
        (lead_factor, True), jnp.dot(lead.T, projected, precision=HIGHEST)
    )
    return matrix - jnp.dot(vectors, coeffs, precision=HIGHEST)


def solution(mesh):
    in_specs = (P("row", "col"),)
    out_specs = P("row", "col")
    return jax.shard_map(
        on_device, mesh=mesh, in_specs=in_specs, out_specs=out_specs, check_vma=False
    )
```

profile of v0, /device:TPU:8, one launch (start us, length us, event | category | flops | bytes accessed | tf_op | source)
XLA Modules:
  0.0 583.5 jit_solution(9986484635231155321)
XLA Ops:
  6.5 7.9 %fusion.1 = f32[256,256]{1,0:T(8,128)S(1)} fusion(f32[3072,384]{1,0:T(8,128)} %param.4), kind=kOutput, calls=%fused_computation.11 | convolution fusion | flops 2415919104 | bytes 3407872 | tf_op jit(solution)/shard_map/dot_general | solution.py:41
  14.7 11.7 %cholesky.256 = f32[128,128]{1,0:T(8,128)S(1)} custom-call(f32[128,128]{1,0:T(8,128)S(1)} %cholesky.422), custom_call_target="Cholesky" | custom-call | tf_op jit(solution)/shard_map/jit(cholesky)/cholesky | solution.py:26
  26.4 9.8 %custom-call.25 = f32[1,128,128]{1,2,0:T(8,128)S(1)} custom-call(f32[1,128,128]{2,1,0:T(8,128)S(1)} %get-tuple-element.77), custom_call_target="InvertDiagBlocksLowerTriangular" | custom-call | tf_op jit(solution)/shard_map/jit(cholesky)/cholesky | solution.py:26
  36.8 11.9 %cholesky.273 = f32[128,128]{1,0:T(8,128)S(1)} custom-call(f32[128,128]{1,0:T(8,128)S(1)} %convolution_subtract_fusion.5), custom_call_target="Cholesky" | custom-call | tf_op jit(solution)/shard_map/jit(cholesky)/cholesky | solution.py:26
  51.3 1.1 collective-permute-done
  53.0 11.7 %cholesky.290 = f32[128,128]{1,0:T(8,128)S(1)} custom-call(f32[128,128]{1,0:T(8,128)S(1)} %cholesky.425), custom_call_target="Cholesky" | custom-call | tf_op jit(solution)/shard_map/jit(cholesky)/cholesky | solution.py:26
  64.8 9.8 %custom-call.26 = f32[1,128,128]{1,2,0:T(8,128)S(1)} custom-call(f32[1,128,128]{2,1,0:T(8,128)S(1)} %get-tuple-element.73), custom_call_target="InvertDiagBlocksLowerTriangular" | custom-call | tf_op jit(solution)/shard_map/jit(cholesky)/cholesky | solution.py:26
  75.1 11.7 %cholesky.307 = f32[128,128]{1,0:T(8,128)S(1)} custom-call(f32[128,128]{1,0:T(8,128)S(1)} %slice_subtract_fusion.2), custom_call_target="Cholesky" | custom-call | tf_op jit(solution)/shard_map/jit(cholesky)/cholesky | solution.py:26
  89.6 2.0 collective-permute-start.1
  91.6 3.8 slice_bitcast_fusion
  95.7 2.7 collective-permute-done.1
  99.0 11.7 %cholesky.324 = f32[128,128]{1,0:T(8,128)S(1)} custom-call(f32[128,128]{1,0:T(8,128)S(1)} %cholesky.428), custom_call_target="Cholesky" | custom-call | tf_op jit(solution)/shard_map/jit(cholesky)/cholesky | solution.py:26
  110.8 9.8 %custom-call.27 = f32[1,128,128]{1,2,0:T(8,128)S(1)} custom-call(f32[1,128,128]{2,1,0:T(8,128)S(1)} %get-tuple-element.69), custom_call_target="InvertDiagBlocksLowerTriangular" | custom-call | tf_op jit(solution)/shard_map/jit(cholesky)/cholesky | solution.py:26
  121.1 11.7 %cholesky.341 = f32[128,128]{1,0:T(8,128)S(1)} custom-call(f32[128,128]{1,0:T(8,128)S(1)} %slice_subtract_fusion.1), custom_call_target="Cholesky" | custom-call | tf_op jit(solution)/shard_map/jit(cholesky)/cholesky | solution.py:26
  135.5 3.3 collective-permute-start.2
  139.2 5.6 collective-permute-done.2
  145.3 11.7 %cholesky.358 = f32[128,128]{1,0:T(8,128)S(1)} custom-call(f32[128,128]{1,0:T(8,128)S(1)} %cholesky.431), custom_call_target="Cholesky" | custom-call | tf_op jit(solution)/shard_map/jit(cholesky)/cholesky | solution.py:26
  157.1 9.8 %custom-call.28 = f32[1,128,128]{1,2,0:T(8,128)S(1)} custom-call(f32[1,128,128]{2,1,0:T(8,128)S(1)} %get-tuple-element.65), custom_call_target="InvertDiagBlocksLowerTriangular" | custom-call | tf_op jit(solution)/shard_map/jit(cholesky)/cholesky | solution.py:26
  167.4 11.7 %cholesky.375 = f32[128,128]{1,0:T(8,128)S(1)} custom-call(f32[128,128]{1,0:T(8,128)S(1)} %slice_subtract_fusion), custom_call_target="Cholesky" | custom-call | tf_op jit(solution)/shard_map/jit(cholesky)/cholesky | solution.py:26
  181.8 4.0 while.3
  182.6 1.3 bitcast_dynamic-update-slice_fusion.4
  184.5 1.3 bitcast_dynamic-update-slice_fusion.4
  185.8 19.7 %custom-call.19 = f32[2,128,128]{1,2,0:T(8,128)S(1)} custom-call(f32[2,128,128]{2,1,0:T(8,128)S(1)} %get-tuple-element.25), custom_call_target="InvertDiagBlocksLowerTriangular" | custom-call | tf_op jit(solution)/shard_map/jit(_solve_triangular)/triangular_solve | solution.py:37
  205.5 2.9 fusion.3
  208.4 5.2 convolution_subtract_fusion.1
  214.0 2.8 fusion.38
  217.9 1.7 copy-done
  219.6 1.9 broadcast_select_fusion
  221.5 66.5 %all-reduce.6.cloned.1.call-done = f32[256,256]{1,0:T(8,128)} async-done(((f32[256,256]{1,0:T(8,128)}), f32[256,256]{1,0:T(8,128)}) %all-reduce.6.cloned.1.call-update) | async-done | bytes 262160 | tf_op jit(solution)/shard_map/psum | solution.py:22
  287.9 1.7 fusion.10
  290.1 159.1 %all-reduce.10.cloned.1.call-done = (f32[3072,256]{1,0:T(8,128)}, f32[256,256]{1,0:T(8,128)}) async-done(((f32[3072,256]{1,0:T(8,128)}, f32[256,256]{1,0:T(8,128)}), (f32[3072,256]{1,0:T(8,128)}, f32[256,256]{1,0:T(8,128)})) %all-reduce.10.cloned.1.call-update) | async-done | bytes 3407888 | tf_op jit(solution)/shard_map/psum | solution.py:22
  449.2 1.8 fusion.78
  453.6 11.7 %cholesky.392 = f32[128,128]{1,0:T(8,128)S(1)} custom-call(f32[128,128]{1,0:T(8,128)S(1)} %cholesky.434), custom_call_target="Cholesky" | custom-call | tf_op jit(solution)/shard_map/jit(cholesky)/cholesky | solution.py:62
  465.3 9.8 %custom-call.29 = f32[1,128,128]{1,2,0:T(8,128)S(1)} custom-call(f32[1,128,128]{2,1,0:T(8,128)S(1)} %get-tuple-element.61), custom_call_target="InvertDiagBlocksLowerTriangular" | custom-call | tf_op jit(solution)/shard_map/jit(cholesky)/cholesky | solution.py:62
  475.1 1.0 constant_dynamic-update-slice_fusion.1
  476.2 1.1 convolution_subtract_fusion.4
  477.3 11.7 %cholesky.409 = f32[128,128]{1,0:T(8,128)S(1)} custom-call(f32[128,128]{1,0:T(8,128)S(1)} %convolution_subtract_fusion.4), custom_call_target="Cholesky" | custom-call | tf_op jit(solution)/shard_map/jit(cholesky)/cholesky | solution.py:62
  490.5 8.0 %fusion.79 = f32[256,384]{1,0:T(8,128)} fusion(f32[3072,256]{1,0:T(8,128)S(1)} %copy-done.1, f32[3072,384]{1,0:T(8,128)} %param.4), kind=kOutput, calls=%fused_computation.151 | convolution fusion | flops 3623878656 | bytes 8257536 | tf_op jit(solution)/shard_map/dot_general | solution.py:59
  499.8 1.7 select_select_fusion
  501.5 5.7 while.4
  502.1 2.2 bitcast_dynamic-update-slice_fusion.5
  505.0 2.2 bitcast_dynamic-update-slice_fusion.5
  507.8 20.5 %custom-call.20 = f32[2,128,128]{1,2,0:T(8,128)S(1)} custom-call(f32[2,128,128]{2,1,0:T(8,128)} %copy-done.5), custom_call_target="InvertDiagBlocksLowerTriangular" | custom-call | tf_op jit(solution)/shard_map/jit(_cho_solve)/triangular_solve | solution.py:63
  528.3 34.7 %all-reduce.8.cloned.1.call-done = f32[256,384]{1,0:T(8,128)} async-done(((f32[256,384]{1,0:T(8,128)}), f32[256,384]{1,0:T(8,128)}) %all-reduce.8.cloned.1.call-update) | async-done | bytes 393232 | tf_op jit(solution)/shard_map/psum | solution.py:60
  563.0 1.6 fusion.80
  565.0 1.2 convolution_subtract_fusion.3
  566.9 1.2 convolution_subtract_fusion.2
  568.4 8.4 %convolution_subtract_fusion = f32[3072,384]{1,0:T(8,128)} fusion(f32[3072,384]{1,0:T(8,128)} %param.4, f32[3072,256]{1,0:T(8,128)S(1)} %copy-done.1, f32[128,384]{1,0:T(8,128)S(1)} %fusion.65, f32[128,384]{1,0:T(8,128)S(1)} %fusion.64), kind=kOutput, calls=%fused_computation.4 | convolution fusion | flops 3625156608 | bytes 12976128 | tf_op jit(solution)/shard_map/dot_general | solution.py:66
  (94 shorter events, 20.8 us)
Async XLA Ops:
  6.5 281.4 %all-reduce.6.cloned.1.call-start = ((), (), s32[]{:S(2)}) async-start(), calls=%async_computation | async-start | bytes 524288 | tf_op jit(solution)/shard_map/psum | solution.py:22
  50.8 1.6 collective-permute-start
  89.6 8.8 %collective-permute-start.1 = (f32[256,256]{0,1:T(8,128)S(1)}, f32[256,256]{0,1:T(8,128)S(1)}, u32[]{:S(2)}, u32[]{:S(2)}) collective-permute-start(f32[256,256]{0,1:T(8,128)S(1)} %fusion.20), channel_id=1, source_target_pairs={{0,64},{64,0},{32,96},{96,32},{128,192},{192,128},{160,224},{224,1... | collective-permute-start | bytes 786440 | tf_op jit(solution)/shard_map/ppermute | solution.py:17
  135.5 9.3 %collective-permute-start.2 = (f32[256,256]{0,1:T(8,128)S(1)}, f32[256,256]{0,1:T(8,128)S(1)}, u32[]{:S(2)}, u32[]{:S(2)}) collective-permute-start(f32[256,256]{0,1:T(8,128)S(1)} %fusion.22), channel_id=1, source_target_pairs={{0,128},{128,0},{32,160},{160,32},{64,192},{192,64},{96,224},{224,... | collective-permute-start | bytes 786440 | tf_op jit(solution)/shard_map/ppermute | solution.py:17
  217.9 1.7 copy-start
  219.5 229.7 %all-reduce.10.cloned.1.call-start = ((), (), s32[]{:S(2)}) async-start(), calls=%async_computation.2 | async-start | bytes 6815744 | tf_op jit(solution)/shard_map/psum | solution.py:22
  289.7 273.3 %all-reduce.8.cloned.1.call-start = ((), (), s32[]{:S(2)}) async-start(), calls=%async_computation.1 | async-start | bytes 786432 | tf_op jit(solution)/shard_map/psum | solution.py:60
  449.2 41.2 %copy-start.1 = (f32[3072,256]{1,0:T(8,128)S(1)}, f32[3072,256]{1,0:T(8,128)}, u32[]{:S(2)}) copy-start(f32[3072,256]{1,0:T(8,128)} %get-tuple-element.50) | copy-start | bytes 9437188
  452.8 0.7 copy-start.4
  489.1 1.4 copy-start.3
  490.5 72.5 %copy-start.2 = (f32[256,256]{1,0:T(8,128)S(1)}, f32[256,256]{1,0:T(8,128)}, u32[]{:S(2)}) copy-start(f32[256,256]{1,0:T(8,128)} %get-tuple-element.51) | copy-start | bytes 786436
  507.2 0.6 copy-start.5
Sparse Core Ops, SparseCore 0:
  219.7 68.2 all-reduce.5
  291.6 157.5 all-reduce.9
  498.6 64.3 all-reduce.7
where the time goes:
time: 593 us; the launch traced here: 583 us
  waiting for transfers between devices  270 us (46%)
  other arithmetic  220 us (37%)
  matrix products  48.8 us (8%)
  between operations  20.2 us (3%)
  local copies, waits for them, and re-layouts  18.1 us (3%)
    psum x2, waiting for transfers between devices, broadcast(): return lax.psum(kept, axis)  226 us
    another operation x27, other arithmetic, upper_of(): return jnp.linalg.cholesky(gram).T  138 us
    another operation x7, other arithmetic, on_device(): lead_factor = jnp.linalg.cholesky(lead_gram)  34.7 us
    psum x1, waiting for transfers between devices, on_device(): projected = lax.psum(partial_proj, 'row')  34.7 us
    another operation x2, other arithmetic, on_device(): jax.scipy.linalg.cho_solve((lead_factor, True), jnp.dot(lead.T, projected...  22.2 us
    another operation x3, other arithmetic, apply_inverse(): return jax.scipy.linalg.solve_triangular(upper.T, rows.T, lower=True).T  19.7 us
  transfers between devices with their start and end apart: 6, of which 6 were waited for; matrix products, arithmetic and copies ran while one was open for 6% of the time, Pallas kernels for 0%

commit v1 on v0

--- a/solution.py
+++ b/solution.py
@@ -5,6 +5,15 @@
 
 PANEL = 256
 HIGHEST = lax.Precision.HIGHEST
+
+
+def sum_by_hops(x, axis):
+    size = lax.axis_size(axis)
+    summed, far = (x, 1)
+    while far < size:
+        summed = summed + lax.ppermute(summed, axis, [(i, i ^ far) for i in range(size)])
+        far = 2 * far
+    return summed
 
 
 def partner_2(block, axis, distance):
@@ -57,7 +66,7 @@
     vectors, lead = factor(panel)
     vectors, lead = (broadcast(vectors, "col", 0), broadcast(lead, "col", 0))
     partial_proj = lax.dot_general(vectors, matrix, (((0,), (0,)), ((), ())), precision=HIGHEST)
-    projected = lax.psum(partial_proj, "row")
+    projected = sum_by_hops(partial_proj, "row")
     lead_gram = jnp.dot(lead.T, lead, precision=HIGHEST)
     lead_factor = jnp.linalg.cholesky(lead_gram)
     coeffs = jax.scipy.linalg.cho_solve(

time: 593 us -> 571 us (0.963)
  waiting for transfers between devices: 270 us -> 242 us
    psum x1 -> x0, waiting for transfers between devices: 34.7 us -> none  [on_device(): projected = lax.psum(partial_proj, 'row')]
    ppermute x0 -> x3, waiting for transfers between devices: none -> 7.08 us  [sum_by_hops(): lax.ppermute(summed, axis, [(i, i ^ far) for i in range(size)])]
  transfers between devices with their start and end apart: 6 -> 8, of which waited for: 6 -> 6; matrix products, arithmetic and copies ran while one was open for 6% -> 8% of each run, Pallas kernels for 0% -> 0%
where the time goes in v1:
time: 571 us; the launch traced here: 560 us
  waiting for transfers between devices  242 us (42%)
  other arithmetic  221 us (39%)
  matrix products  47.8 us (8%)
  between operations  20.8 us (4%)
  local copies, waits for them, and re-layouts  16.7 us (3%)
  starting transfers between devices  10.1 us (2%)
    psum x2, waiting for transfers between devices, broadcast(): return lax.psum(kept, axis)  226 us
    another operation x27, other arithmetic, upper_of(): return jnp.linalg.cholesky(gram).T  138 us
    another operation x7, other arithmetic, on_device(): lead_factor = jnp.linalg.cholesky(lead_gram)  34.6 us
    another operation x2, other arithmetic, on_device(): jax.scipy.linalg.cho_solve((lead_factor, True), jnp.dot(lead.T, projected...  21.2 us
    another operation x3, other arithmetic, apply_inverse(): return jax.scipy.linalg.solve_triangular(upper.T, rows.T, lower=True).T  19.7 us
  transfers between devices with their start and end apart: 8, of which 6 were waited for; matrix products, arithmetic and copies ran while one was open for 8% of the time, Pallas kernels for 0%

profile of v1, /device:TPU:8, one launch (start us, length us, event | category | flops | bytes accessed | tf_op | source)
XLA Modules:
  0.0 559.6 jit_solution(2932024004785954082)
XLA Ops:
  6.5 7.9 %fusion.1 = f32[256,256]{1,0:T(8,128)S(1)} fusion(f32[3072,384]{1,0:T(8,128)} %param.4), kind=kOutput, calls=%fused_computation.11 | convolution fusion | flops 2415919104 | bytes 3407872 | tf_op jit(solution)/shard_map/dot_general | solution.py:50
  14.7 11.7 %cholesky.256 = f32[128,128]{1,0:T(8,128)S(1)} custom-call(f32[128,128]{1,0:T(8,128)S(1)} %cholesky.422), custom_call_target="Cholesky" | custom-call | tf_op jit(solution)/shard_map/jit(cholesky)/cholesky | solution.py:35
  26.4 9.8 %custom-call.25 = f32[1,128,128]{1,2,0:T(8,128)S(1)} custom-call(f32[1,128,128]{2,1,0:T(8,128)S(1)} %get-tuple-element.77), custom_call_target="InvertDiagBlocksLowerTriangular" | custom-call | tf_op jit(solution)/shard_map/jit(cholesky)/cholesky | solution.py:35
  36.8 12.1 %cholesky.273 = f32[128,128]{1,0:T(8,128)S(1)} custom-call(f32[128,128]{1,0:T(8,128)S(1)} %convolution_subtract_fusion.4), custom_call_target="Cholesky" | custom-call | tf_op jit(solution)/shard_map/jit(cholesky)/cholesky | solution.py:35
  51.5 1.1 collective-permute-done
  53.2 11.7 %cholesky.290 = f32[128,128]{1,0:T(8,128)S(1)} custom-call(f32[128,128]{1,0:T(8,128)S(1)} %cholesky.425), custom_call_target="Cholesky" | custom-call | tf_op jit(solution)/shard_map/jit(cholesky)/cholesky | solution.py:35
  65.0 9.8 %custom-call.26 = f32[1,128,128]{1,2,0:T(8,128)S(1)} custom-call(f32[1,128,128]{2,1,0:T(8,128)S(1)} %get-tuple-element.73), custom_call_target="InvertDiagBlocksLowerTriangular" | custom-call | tf_op jit(solution)/shard_map/jit(cholesky)/cholesky | solution.py:35
  75.3 11.7 %cholesky.307 = f32[128,128]{1,0:T(8,128)S(1)} custom-call(f32[128,128]{1,0:T(8,128)S(1)} %slice_subtract_fusion.4), custom_call_target="Cholesky" | custom-call | tf_op jit(solution)/shard_map/jit(cholesky)/cholesky | solution.py:35
  89.7 1.7 collective-permute-start.1
  91.5 3.8 slice_bitcast_fusion
  95.7 2.7 collective-permute-done.1
  99.0 11.7 %cholesky.324 = f32[128,128]{1,0:T(8,128)S(1)} custom-call(f32[128,128]{1,0:T(8,128)S(1)} %cholesky.428), custom_call_target="Cholesky" | custom-call | tf_op jit(solution)/shard_map/jit(cholesky)/cholesky | solution.py:35
  110.7 9.8 %custom-call.27 = f32[1,128,128]{1,2,0:T(8,128)S(1)} custom-call(f32[1,128,128]{2,1,0:T(8,128)S(1)} %get-tuple-element.69), custom_call_target="InvertDiagBlocksLowerTriangular" | custom-call | tf_op jit(solution)/shard_map/jit(cholesky)/cholesky | solution.py:35
  121.0 11.7 %cholesky.341 = f32[128,128]{1,0:T(8,128)S(1)} custom-call(f32[128,128]{1,0:T(8,128)S(1)} %slice_subtract_fusion.3), custom_call_target="Cholesky" | custom-call | tf_op jit(solution)/shard_map/jit(cholesky)/cholesky | solution.py:35
  135.4 3.3 collective-permute-start.2
  139.2 5.5 collective-permute-done.2
  145.3 11.7 %cholesky.358 = f32[128,128]{1,0:T(8,128)S(1)} custom-call(f32[128,128]{1,0:T(8,128)S(1)} %cholesky.431), custom_call_target="Cholesky" | custom-call | tf_op jit(solution)/shard_map/jit(cholesky)/cholesky | solution.py:35
  157.1 9.8 %custom-call.28 = f32[1,128,128]{1,2,0:T(8,128)S(1)} custom-call(f32[1,128,128]{2,1,0:T(8,128)S(1)} %get-tuple-element.65), custom_call_target="InvertDiagBlocksLowerTriangular" | custom-call | tf_op jit(solution)/shard_map/jit(cholesky)/cholesky | solution.py:35
  167.4 11.7 %cholesky.375 = f32[128,128]{1,0:T(8,128)S(1)} custom-call(f32[128,128]{1,0:T(8,128)S(1)} %slice_subtract_fusion.2), custom_call_target="Cholesky" | custom-call | tf_op jit(solution)/shard_map/jit(cholesky)/cholesky | solution.py:35
  181.8 4.2 while.3
  182.8 1.3 bitcast_dynamic-update-slice_fusion.4
  184.7 1.3 bitcast_dynamic-update-slice_fusion.4
  186.0 19.7 %custom-call.19 = f32[2,128,128]{1,2,0:T(8,128)S(1)} custom-call(f32[2,128,128]{2,1,0:T(8,128)S(1)} %get-tuple-element.25), custom_call_target="InvertDiagBlocksLowerTriangular" | custom-call | tf_op jit(solution)/shard_map/jit(_solve_triangular)/triangular_solve | solution.py:46
  205.7 2.9 fusion.3
  208.6 5.2 convolution_subtract_fusion.1
  214.2 2.8 fusion.41
  218.0 1.7 copy-done
  219.9 1.9 broadcast_select_fusion
  221.8 66.3 %all-reduce.5.cloned.1.call-done = f32[256,256]{1,0:T(8,128)} async-done(((f32[256,256]{1,0:T(8,128)}), f32[256,256]{1,0:T(8,128)}) %all-reduce.5.cloned.1.call-update) | async-done | bytes 262160 | tf_op jit(solution)/shard_map/psum | solution.py:31
  288.1 1.7 fusion.12
  289.8 159.6 %all-reduce.7.cloned.1.call-done = (f32[3072,256]{1,0:T(8,128)}, f32[256,256]{1,0:T(8,128)}) async-done(((f32[3072,256]{1,0:T(8,128)}, f32[256,256]{1,0:T(8,128)}), (f32[3072,256]{1,0:T(8,128)}, f32[256,256]{1,0:T(8,128)})) %all-reduce.7.cloned.1.call-update) | async-done | bytes 3407888 | tf_op jit(solution)/shard_map/psum | solution.py:31
  449.4 1.6 fusion.81
  451.2 11.7 %cholesky.392 = f32[128,128]{1,0:T(8,128)S(1)} custom-call(f32[128,128]{1,0:T(8,128)S(1)} %cholesky.434), custom_call_target="Cholesky" | custom-call | tf_op jit(solution)/shard_map/jit(cholesky)/cholesky | solution.py:71
  463.0 9.8 %custom-call.29 = f32[1,128,128]{1,2,0:T(8,128)S(1)} custom-call(f32[1,128,128]{2,1,0:T(8,128)S(1)} %get-tuple-element.61), custom_call_target="InvertDiagBlocksLowerTriangular" | custom-call | tf_op jit(solution)/shard_map/jit(cholesky)/cholesky | solution.py:71
  472.8 8.7 %fusion.82 = f32[256,384]{1,0:T(8,128)S(1)} fusion(f32[3072,256]{1,0:T(8,128)} %get-tuple-element.50, f32[3072,384]{1,0:T(8,128)} %param.4), kind=kOutput, calls=%fused_computation.154 | convolution fusion | flops 3623878656 | bytes 8257536 | tf_op jit(solution)/shard_map/dot_general | solution.py:68
  482.1 11.7 %cholesky.409 = f32[128,128]{1,0:T(8,128)S(1)} custom-call(f32[128,128]{1,0:T(8,128)S(1)} %convolution_subtract_fusion.3), custom_call_target="Cholesky" | custom-call | tf_op jit(solution)/shard_map/jit(cholesky)/cholesky | solution.py:71
  494.7 1.5 collective-permute-start.4
  499.4 7.1 %collective-permute-done.4 = f32[256,384]{1,0:T(8,128)} collective-permute-done((f32[256,384]{1,0:T(8,128)}, f32[256,384]{1,0:T(8,128)}, u32[]{:S(2)}, u32[]{:S(2)}) %collective-permute-start.4) | collective-permute-done | bytes 393248 | tf_op jit(solution)/shard_map/ppermute | solution.py:14
  506.5 1.9 add.65
  508.4 3.2 collective-permute-start.5
  511.6 5.6 while.4
  512.3 2.2 bitcast_dynamic-update-slice_fusion.5
  515.1 2.1 bitcast_dynamic-update-slice_fusion.5
  517.9 20.5 %custom-call.20 = f32[2,128,128]{1,2,0:T(8,128)S(1)} custom-call(f32[2,128,128]{2,1,0:T(8,128)} %copy-done.3), custom_call_target="InvertDiagBlocksLowerTriangular" | custom-call | tf_op jit(solution)/shard_map/jit(_cho_solve)/triangular_solve | solution.py:72
  538.4 1.7 fusion.8
  540.5 1.2 fusion.70
  542.4 1.2 convolution_subtract_fusion.2
  543.9 8.4 %convolution_subtract_fusion = f32[3072,384]{1,0:T(8,128)} fusion(f32[3072,384]{1,0:T(8,128)} %param.4, f32[3072,256]{1,0:T(8,128)S(1)} %copy-done.1, f32[128,384]{1,0:T(8,128)S(1)} %fusion.68, f32[128,384]{1,0:T(8,128)S(1)} %fusion.67), kind=kOutput, calls=%fused_computation.4 | convolution fusion | flops 3625156608 | bytes 12976128 | tf_op jit(solution)/shard_map/dot_general | solution.py:75
  (95 shorter events, 20.2 us)
Async XLA Ops:
  6.5 281.6 %all-reduce.5.cloned.1.call-start = ((), (), s32[]{:S(2)}) async-start(), calls=%async_computation | async-start | bytes 524288 | tf_op jit(solution)/shard_map/psum | solution.py:31
  51.0 1.6 collective-permute-start
  89.7 8.6 %collective-permute-start.1 = (f32[256,256]{0,1:T(8,128)S(1)}, f32[256,256]{0,1:T(8,128)S(1)}, u32[]{:S(2)}, u32[]{:S(2)}) collective-permute-start(f32[256,256]{0,1:T(8,128)S(1)} %fusion.22), channel_id=1, source_target_pairs={{0,64},{64,0},{32,96},{96,32},{128,192},{192,128},{160,224},{224,1... | collective-permute-start | bytes 786440 | tf_op jit(solution)/shard_map/ppermute | solution.py:26
  135.4 9.3 %collective-permute-start.2 = (f32[256,256]{0,1:T(8,128)S(1)}, f32[256,256]{0,1:T(8,128)S(1)}, u32[]{:S(2)}, u32[]{:S(2)}) collective-permute-start(f32[256,256]{0,1:T(8,128)S(1)} %fusion.24), channel_id=1, source_target_pairs={{0,128},{128,0},{32,160},{160,32},{64,192},{192,64},{96,224},{224,... | collective-permute-start | bytes 786440 | tf_op jit(solution)/shard_map/ppermute | solution.py:26
  218.0 1.7 copy-start
  219.7 229.7 %all-reduce.7.cloned.1.call-start = ((), (), s32[]{:S(2)}) async-start(), calls=%async_computation.1 | async-start | bytes 6815744 | tf_op jit(solution)/shard_map/psum | solution.py:31
  481.5 56.8 %copy-start.2 = (f32[256,256]{1,0:T(8,128)S(1)}, f32[256,256]{1,0:T(8,128)}, u32[]{:S(2)}) copy-start(f32[256,256]{1,0:T(8,128)} %get-tuple-element.51) | copy-start | bytes 786436
  481.5 12.3 %collective-permute-start.3 = (f32[256,384]{1,0:T(8,128)S(1)}, f32[256,384]{1,0:T(8,128)S(1)}, u32[]{:S(2)}, u32[]{:S(2)}) collective-permute-start(f32[256,384]{1,0:T(8,128)S(1)} %fusion.82), channel_id=1, source_target_pairs={{0,32},{32,0},{64,96},{96,64},{128,160},{160,128},{192,224},{224,1... | collective-permute-start | bytes 1179656 | tf_op jit(solution)/shard_map/ppermute | solution.py:14
  494.7 11.8 %collective-permute-start.4 = (f32[256,384]{1,0:T(8,128)}, f32[256,384]{1,0:T(8,128)}, u32[]{:S(2)}, u32[]{:S(2)}) collective-permute-start(f32[256,384]{1,0:T(8,128)} %add.64), channel_id=1, source_target_pairs={{0,64},{32,96},{64,0},{96,32},{128,192},{160,224},{192,128},{224,1... | collective-permute-start | bytes 1179656 | tf_op jit(solution)/shard_map/ppermute | solution.py:14
  499.4 44.5 %copy-start.1 = (f32[3072,256]{1,0:T(8,128)S(1)}, f32[3072,256]{1,0:T(8,128)}, u32[]{:S(2)}) copy-start(f32[3072,256]{1,0:T(8,128)} %get-tuple-element.50) | copy-start | bytes 9437188
  508.4 30.0 %collective-permute-start.5 = (f32[256,384]{1,0:T(8,128)}, f32[256,384]{1,0:T(8,128)}, u32[]{:S(2)}, u32[]{:S(2)}) collective-permute-start(f32[256,384]{1,0:T(8,128)} %add.65), channel_id=1, source_target_pairs={{0,128},{32,160},{64,192},{96,224},{128,0},{160,32},{192,64},{224,... | collective-permute-start | bytes 1179656 | tf_op jit(solution)/shard_map/ppermute | solution.py:14
  517.2 0.7 copy-start.3
Sparse Core Ops, SparseCore 0:
  219.8 68.2 all-reduce.4
  291.8 157.5 all-reduce.6
